TPU v7x, 32 devices: a whole 2x2x4 slice. The times are simulated.
32 devices in a mesh: dp: 8 (over z, y), tensor: 4 (over x, core).
Axes of the slice: x: 2, y: 2, z: 4, core: 2. Of those that a mesh axis runs over, the one named last changes fastest.
Arguments:
- tokens: bfloat16 [8192, 1536], P('dp', 'tensor'), may hold values from -6 to 6
- segments: int32 [8, 1024], P('dp'), may hold values from 0 to 7, never falling along the last dimension, each value on 1 to 512 neighbouring positions
- attn_gain: bfloat16 [1536], P('tensor'), may hold values from 0.25 to 1.75
- w_qkv: bfloat16 [3, 1536, 1536], P(None, None, 'tensor'), may hold values from -0.15625 to 0.15625
- kq_kernel: float32 [16, 6, 11], P('tensor'), may hold values from -0.8 to 1.8
- head_mix: float32 [16, 2], P('tensor'), may hold values from -0.6 to 1.3
- group_gain: bfloat16 [1536], P('tensor'), may hold values from 0.25 to 1.75
- w_out: bfloat16 [1536, 1536], P('tensor'), may hold values from -0.15625 to 0.15625
- mlp_gain: bfloat16 [1536], P('tensor'), may hold values from 0.25 to 1.75
- w_gate_up: bfloat16 [2, 1536, 4096], P(None, None, 'tensor'), may hold values from -0.15625 to 0.15625
- w_down: bfloat16 [4096, 1536], P('tensor'), may hold values from -0.09375 to 0.09375
- cotangent: bfloat16 [8192, 1536], P('dp', 'tensor'), may hold values from -6 to 6
Outputs:
- layer_out: bfloat16 [8192, 1536], P('dp', 'tensor')
- tokens_grad: float32 [8192, 1536], P('dp', 'tensor')
- attn_gain_grad: float32 [1536], P('tensor')
- w_qkv_grad: float32 [3, 1536, 1536], P(None, None, 'tensor')
- kq_kernel_grad: float32 [16, 6, 11], P('tensor')
- head_mix_grad: float32 [16, 2], P('tensor')
- group_gain_grad: float32 [1536], P('tensor')
- w_out_grad: float32 [1536, 1536], P('tensor')
- mlp_gain_grad: float32 [1536], P('tensor')
- w_gate_up_grad: float32 [2, 1536, 4096], P(None, None, 'tensor')
- w_down_grad: float32 [4096, 1536], P('tensor')
Inputs may be any that keep to these rules, and one draw needn't show every extreme that they name: `segments`: within a sequence the numbers never fall; each document holds at most 512 tokens.
All inputs are finite; a program needn't handle non-finite values.
Results may differ from a plain program's by a relative error of at most 0.018.
The roundings to bfloat16 on the way count: a program that leaves them out, or rounds other values in their place, can miss the bound.
Values may be sent and summed in bfloat16 or wider, within the bound.
A program may use at most 320 MiB of HBM per device.

v0:
```python
import jax
import jax.numpy as jnp
from jax import lax
from jax.sharding import PartitionSpec as P

HEAD_DIM = 96
EPS = 1e-05
NEG = -1e30
HIGH = lax.Precision.HIGHEST


def valid_pairs(seg_row):
    length = seg_row.shape[0]
    place = lax.iota(jnp.int32, length)
    return (place[None, :] <= place[:, None]) & (seg_row[:, None] == seg_row[None, :])


def padded_scores(masked, kernel):
    query_taps = kernel.shape[1]
    key_half = kernel.shape[2] // 2
    return jnp.pad(masked, ((0, 0), (query_taps - 1, 0), (key_half, key_half)))


def conv_window(padded, kernel, query_shift, key_shift, length):
    query_taps = kernel.shape[1]
    key_taps = kernel.shape[2]
    row_start = query_taps - 1 - query_shift
    col_start = key_taps - 1 - key_shift
    return lax.slice(
        padded, (0, row_start, col_start), (padded.shape[0], row_start + length, col_start + length)
    )


def kq_conv(masked, kernel):
    length = masked.shape[1]
    padded = padded_scores(masked, kernel)
    summed = jnp.zeros(masked.shape, jnp.float32)
    for query_shift in range(kernel.shape[1]):
        for key_shift in range(kernel.shape[2]):
            shifted = conv_window(padded, kernel, query_shift, key_shift, length)
            summed = summed + kernel[:, query_shift, key_shift][:, None, None] * shifted
    return summed


def conv_back(grad_logits, masked, kernel):
    query_taps = kernel.shape[1]
    key_taps = kernel.shape[2]
    key_half = key_taps // 2
    heads_here = masked.shape[0]
    length = masked.shape[1]
    padded_in = padded_scores(masked, kernel)
    padded_grad = jnp.pad(grad_logits, ((0, 0), (0, query_taps - 1), (key_half, key_half)))
    grad_masked = jnp.zeros(masked.shape, jnp.float32)
    kernel_terms = []
    for query_shift in range(query_taps):
        for key_shift in range(key_taps):
            window_in = conv_window(padded_in, kernel, query_shift, key_shift, length)
            window_grad = lax.slice(
                padded_grad,
                (0, query_shift, key_shift),
                (heads_here, query_shift + length, key_shift + length),
            )
            grad_masked = (
                grad_masked + kernel[:, query_shift, key_shift][:, None, None] * window_grad
            )
            kernel_terms.append(jnp.sum(grad_logits * window_in, axis=(1, 2)))
    grad_kernel = jnp.stack(kernel_terms, axis=1).reshape(heads_here, query_taps, key_taps)
    return (grad_masked, grad_kernel)


def mix_heads(probs, mix):
    heads_here = probs.shape[0]
    length = probs.shape[1]
    paired = probs.reshape(heads_here // 2, 2, length, length)
    weights = mix.reshape(heads_here // 2, 2, 2)
    first = weights[:, :, 0][:, :, None, None] * paired[:, 0][:, None]
    second = weights[:, :, 1][:, :, None, None] * paired[:, 1][:, None]
    return (first + second).reshape(heads_here, length, length)


def mix_back(grad_mixed, probs, mix):
    heads_here = probs.shape[0]
    length = probs.shape[1]
    paired_grad = grad_mixed.reshape(heads_here // 2, 2, length, length)
    paired = probs.reshape(heads_here // 2, 2, length, length)
    weights = mix.reshape(heads_here // 2, 2, 2)
    grad_probs = (
        weights[:, 0, :][:, :, None, None] * paired_grad[:, 0][:, None]
        + weights[:, 1, :][:, :, None, None] * paired_grad[:, 1][:, None]
    )
    grad_mix = jnp.einsum("grqk,gsqk->grs", paired_grad, paired, precision=HIGH)
    return (grad_probs.reshape(heads_here, length, length), grad_mix.reshape(heads_here, 2))


def score_logits(query, keys, seg_row, kernel):
    scale = query.shape[2] ** (-0.5)
    valid = valid_pairs(seg_row)[None]
    raw = jnp.einsum("qhd,khd->hqk", query, keys, preferred_element_type=jnp.float32)
    masked = jnp.where(valid, raw * scale, 0.0)
    logits = jnp.where(valid, kq_conv(masked, kernel), NEG)
    return (valid, masked, logits)


def attend_forward(query, keys, values, seg_row, kernel, mix):
    valid, masked, logits = score_logits(query, keys, seg_row, kernel)
    peak = jnp.max(logits, axis=-1, keepdims=True)
    expo = jnp.exp(logits - peak)
    summed = jnp.sum(expo, axis=-1, keepdims=True)
    probs = expo / summed
    mixed = mix_heads(probs, mix).astype(jnp.bfloat16)
    output = jnp.einsum("hqk,khd->qhd", mixed, values, preferred_element_type=jnp.float32)
    return (output, (peak + jnp.log(summed))[..., 0])


def attend_backward(query, keys, values, seg_row, grad_out, log_norm, kernel, mix):
    scale = query.shape[2] ** (-0.5)
    valid, masked, logits = score_logits(query, keys, seg_row, kernel)
    probs = jnp.exp(logits - log_norm[..., None])
    mixed = mix_heads(probs, mix).astype(jnp.bfloat16)
    grad_values = jnp.einsum("hqk,qhd->khd", mixed, grad_out, preferred_element_type=jnp.float32)
    grad_mixed = jnp.einsum("qhd,khd->hqk", grad_out, values, preferred_element_type=jnp.float32)
    grad_probs, grad_mix = mix_back(grad_mixed, probs, mix)
    grad_logits = probs * (grad_probs - jnp.sum(grad_probs * probs, axis=-1, keepdims=True))
    grad_masked, grad_kernel = conv_back(grad_logits, masked, kernel)
    grad_scores = (jnp.where(valid, grad_masked, 0.0) * scale).astype(jnp.bfloat16)
    grad_query = jnp.einsum("hqk,khd->qhd", grad_scores, keys, preferred_element_type=jnp.float32)
    grad_keys = jnp.einsum("hqk,qhd->khd", grad_scores, query, preferred_element_type=jnp.float32)
    return (grad_query, grad_keys, grad_values, grad_kernel, grad_mix)


def contract_rows(left, right):
    return lax.dot_general(
        left, right, (((0,), (0,)), ((), ())), preferred_element_type=jnp.float32
    )


def contract_cols(left, right):
    return lax.dot_general(
        left, right, (((1,), (1,)), ((), ())), preferred_element_type=jnp.float32
    )


def on_device(
    tokens,
    segments,
    attn_gain,
    w_qkv,
    kq_kernel,
    head_mix,
    group_gain,
    w_out,
    mlp_gain,
    w_gate_up,
    w_down,
    cotangent,
):
    rank = lax.axis_index("tensor")
    rows_here = tokens.shape[0]
    local_width = tokens.shape[1]
    seq_count = segments.shape[0]
    length = segments.shape[1]
    heads_here = w_qkv.shape[2] // HEAD_DIM
    start = rank * local_width
    gathered, gain_one, gain_two = (
        lax.all_gather(tokens, "tensor", axis=1, tiled=True),
        lax.all_gather(attn_gain, "tensor", axis=0, tiled=True),
        lax.all_gather(mlp_gain, "tensor", axis=0, tiled=True),
    )
    resid = gathered.astype(jnp.float32)
    full_width = resid.shape[1]
    scale_one = lax.rsqrt(jnp.mean(resid * resid, axis=-1, keepdims=True) + EPS)
    unit_one = resid * scale_one
    normed_one = (unit_one * gain_one.astype(jnp.float32)).astype(jnp.bfloat16)
    projected = jnp.einsum(
        "td,cde->cte", normed_one, w_qkv, preferred_element_type=jnp.float32
    ).astype(jnp.bfloat16)
    split_heads = projected.reshape(3, seq_count, length, heads_here, HEAD_DIM)

    def forward_one(items):
        return attend_forward(items[0], items[1], items[2], items[3], kq_kernel, head_mix)

    heads_out, log_norms = lax.map(
        forward_one, (split_heads[0], split_heads[1], split_heads[2], segments)
    )
    heads_out = heads_out.reshape(rows_here, heads_here, HEAD_DIM)
    group_scale = lax.rsqrt(jnp.mean(heads_out * heads_out, axis=-1, keepdims=True) + EPS)
    unit_heads = heads_out * group_scale
    gain_heads = group_gain.astype(jnp.float32).reshape(heads_here, HEAD_DIM)
    grouped = (unit_heads * gain_heads).astype(jnp.bfloat16).reshape(rows_here, local_width)
    attn_part = jnp.dot(grouped, w_out, preferred_element_type=jnp.float32)
    gain_full = gain_two.astype(jnp.float32)
    attn = lax.psum(attn_part, "tensor")
    hidden = resid + attn
    scale_two = lax.rsqrt(jnp.mean(hidden * hidden, axis=-1, keepdims=True) + EPS)
    unit_two = hidden * scale_two
    normed_two = (unit_two * gain_full).astype(jnp.bfloat16)
    hidden_local = lax.dynamic_slice_in_dim(hidden, start, local_width, 1)
    gate_up = jnp.einsum("td,cdf->ctf", normed_two, w_gate_up, preferred_element_type=jnp.float32)
    gate = gate_up[0]
    up = gate_up[1]
    sigmoid = jax.nn.sigmoid(gate)
    swish = gate * sigmoid
    act = (swish * up).astype(jnp.bfloat16)
    mlp_part = jnp.dot(act, w_down, preferred_element_type=jnp.float32)
    mlp_local = lax.psum_scatter(
        mlp_part.astype(jnp.bfloat16), "tensor", scatter_dimension=1, tiled=True
    ).astype(jnp.float32)
    layer_out = (hidden_local + mlp_local).astype(jnp.bfloat16)
    full_cot = lax.all_gather(cotangent, "tensor", axis=1, tiled=True)
    grad_down = contract_rows(act, full_cot)
    grad_act = contract_cols(full_cot, w_down)
    grad_gate = grad_act * up * sigmoid * (1.0 + gate * (1.0 - sigmoid))
    grad_up = grad_act * swish
    grad_pair = jnp.stack([grad_gate, grad_up]).astype(jnp.bfloat16)
    grad_gate_up = jnp.einsum(
        "td,ctf->cdf", normed_two, grad_pair, preferred_element_type=jnp.float32
    )
    grad_two_part = jnp.einsum(
        "ctf,cdf->td", grad_pair, w_gate_up, preferred_element_type=jnp.float32
    )
    grad_two = lax.psum(grad_two_part, "tensor")
    grad_gain_two = lax.dynamic_slice_in_dim(
        jnp.sum(grad_two * unit_two, axis=0), start, local_width, 0
    )
    scaled_two = grad_two * gain_full
    grad_hidden = full_cot.astype(jnp.float32) + scale_two * (
        scaled_two - unit_two * jnp.mean(scaled_two * unit_two, axis=-1, keepdims=True)
    )
    grad_attn = grad_hidden.astype(jnp.bfloat16)
    grad_hidden_local = lax.dynamic_slice_in_dim(grad_hidden, start, local_width, 1)
    grad_w_out = contract_rows(grouped, grad_attn)
    grad_grouped = contract_cols(grad_attn, w_out).reshape(rows_here, heads_here, HEAD_DIM)
    grad_group_gain = jnp.sum(grad_grouped * unit_heads, axis=0).reshape(local_width)
    scaled_heads = grad_grouped * gain_heads
    grad_heads = (
        group_scale
        * (scaled_heads - unit_heads * jnp.mean(scaled_heads * unit_heads, axis=-1, keepdims=True))
    ).astype(jnp.bfloat16)
    grad_split = grad_heads.reshape(seq_count, length, heads_here, HEAD_DIM)

    def backward_one(items):
        return attend_backward(
            items[0], items[1], items[2], items[3], items[4], items[5], kq_kernel, head_mix
        )

    grad_query, grad_keys, grad_values, kernel_terms, mix_terms = lax.map(
        backward_one,
        (split_heads[0], split_heads[1], split_heads[2], segments, grad_split, log_norms),
    )
    grad_proj = (
        jnp.stack([grad_query, grad_keys, grad_values])
        .astype(jnp.bfloat16)
        .reshape(3, rows_here, local_width)
    )
    grad_kernel = jnp.sum(kernel_terms, axis=0)
    grad_mix = jnp.sum(mix_terms, axis=0)
    grad_qkv = jnp.einsum("td,cte->cde", normed_one, grad_proj, preferred_element_type=jnp.float32)
    grad_one_part = jnp.einsum("cte,cde->td", grad_proj, w_qkv, preferred_element_type=jnp.float32)
    grad_one = lax.psum_scatter(
        grad_one_part.astype(jnp.bfloat16), "tensor", scatter_dimension=1, tiled=True
    ).astype(jnp.float32)
    unit_local = lax.dynamic_slice_in_dim(unit_one, start, local_width, 1)
    scaled_one = grad_one * attn_gain.astype(jnp.float32)
    row_total = lax.psum(jnp.sum(scaled_one * unit_local, axis=-1, keepdims=True), "tensor")
    tokens_grad = grad_hidden_local + scale_one * (
        scaled_one - unit_local * (row_total / full_width)
    )
    grad_gain_one = jnp.sum(grad_one * unit_local, axis=0)
    (
        grad_gain_one,
        grad_qkv,
        grad_kernel,
        grad_mix,
        grad_group_gain,
        grad_w_out,
        grad_gain_two,
        grad_gate_up,
        grad_down,
    ) = lax.psum(
        (
            grad_gain_one,
            grad_qkv,
            grad_kernel,
            grad_mix,
            grad_group_gain,
            grad_w_out,
            grad_gain_two,
            grad_gate_up,
            grad_down,
        ),
        "dp",
    )
    return (
        layer_out,
        tokens_grad,
        grad_gain_one,
        grad_qkv,
        grad_kernel,
        grad_mix,
        grad_group_gain,
        grad_w_out,
        grad_gain_two,
        grad_gate_up,
        grad_down,
    )


def solution(mesh):
    in_specs = (
        P("dp", "tensor"),
        P("dp", None),
        P("tensor"),
        P(None, None, "tensor"),
        P("tensor", None, None),
        P("tensor", None),
        P("tensor"),
        P("tensor", None),
        P("tensor"),
        P(None, None, "tensor"),
        P("tensor", None),
        P("dp", "tensor"),
    )
    out_specs = (
        P("dp", "tensor"),
        P("dp", "tensor"),
        P("tensor"),
        P(None, None, "tensor"),
        P("tensor", None, None),
        P("tensor", None),
        P("tensor"),
        P("tensor", None),
        P("tensor"),
        P(None, None, "tensor"),
        P("tensor", None),
    )
    return jax.shard_map(
        on_device, mesh=mesh, in_specs=in_specs, out_specs=out_specs, check_vma=False
    )
```

profile of v0, /device:TPU:0, one launch (start us, length us, event | category | flops | bytes accessed | tf_op | source)
XLA Modules:
  0.0 3078.3 jit_solution(3075463424177838024)
XLA Ops:
  29.7 11.2 all-gather.5.cloned.1.call-done
  50.7 8.6 multiply_select_fusion
  59.3 754.6 %fusion.168 = (f32[4,1024]{1,0:T(4,128)S(1)}, f32[4,1024,1024]{2,1,0:T(8,128)}) fusion(f32[4]{0:T(128)} %get-tuple-element.249, f32[4]{0:T(128)} %get-tuple-element.250, f32[4]{0:T(128)} %get-tuple-element.186, f32[4]{0:T(128)} %get-tuple-element.187, f32[4]{0:T(128)} %get-tuple-element.188, f32[4]{0:T(128)} %get-tuple-element.189, ...), kind=kLoop, calls=%fused_computation.489 | loop fusion | flops 557838336 | bytes 34620448 | tf_op jit(solution)/shard_map/while/body/eval_jaxpr/reduce_max | solution.py:106
  813.9 7.8 fusion.140
  829.3 7.6 slice_bitcast_fusion.5
  836.9 7.4 fusion.138
  862.4 111.2 %all-reduce.8.cloned.1.call-done = f32[1024,1536]{1,0:T(8,128)} async-done(((f32[1024,1536]{1,0:T(8,128)}), f32[1024,1536]{1,0:T(8,128)}) %all-reduce.8.cloned.1.call-update) | async-done | bytes 6291472 | tf_op jit(solution)/shard_map/psum | solution.py:192
  973.6 7.6 multiply_reduce_fusion.68
  984.2 11.3 convolution_bitcast_fusion.3
  995.5 8.4 all-gather.7.cloned.1.call-done
  1003.9 11.5 fusion.147
  1017.4 10.5 convolution_bitcast_fusion.2
  1035.9 7.6 convolution_convert_fusion
  1048.3 99.3 %all-reduce.10.cloned.1.call-done = f32[1024,1536]{1,0:T(8,128)} async-done(((f32[1024,1536]{1,0:T(8,128)}), f32[1024,1536]{1,0:T(8,128)}) %all-reduce.10.cloned.1.call-update) | async-done | bytes 6291472 | tf_op jit(solution)/shard_map/psum | solution.py:221
  1166.3 7.1 slice_bitcast_fusion.3
  1177.5 21.4 fusion.134
  1199.0 101.0 %multiply_reduce_fusion.54 = (f32[4]{0:T(128)}, f32[4]{0:T(128)}, f32[4]{0:T(128)}, f32[4]{0:T(128)}, f32[4]{0:T(128)}, /*index=5*/f32[4]{0:T(128)}, f32[4]{0:T(...) fusion(f32[4,1024,1024]{2,1,0:T(8,128)} %multiply_select_fusion, ...), kind=kOutput, calls=%fused_computation.329 | output fusion | flops 121639920 | bytes 83886304 | tf_op jit(solution)/shard_map/while/body/eval_jaxpr/sub | solution.py:123
  1300.0 771.0 %multiply_convert_fusion = bf16[4,1024,1024]{2,1,0:T(8,128)(2,1)} fusion(f32[4,1024,1024]{2,1,0:T(8,128)} %get-tuple-element.285, f32[4]{0:T(128)} %get-tuple-element.249, f32[4]{0:T(128)} %get-tuple-element.250, f32[4]{0:T(128)} %get-tuple-element.186, f32[4]{0:T(128)} %get-tuple-element.187, f32[4]{0:T(128)} %get-tuple-element.188, ...), kind=kLoop, calls=%fused_computation.341 | loop fusion | flops 562036736 | bytes 26215456 | tf_op jit(solution)/shard_map/while/body/eval_jaxpr/convert_element_type | solution.py:125
  2071.0 7.2 convolution_convert_fusion.3
  2088.8 6.7 slice_bitcast_fusion.1
  2103.1 7.3 bitcast_convert_fusion
  2115.1 9.1 fusion.175
  2124.2 13.9 convolution_bitcast_fusion
  2148.6 25.6 copy.125
  2174.2 25.6 copy.126
  2211.7 181.0 %multiply_reduce_fusion.36 = (f32[4]{0:T(128)}, f32[4]{0:T(128)}, f32[4]{0:T(128)}, f32[4]{0:T(128)}, f32[4]{0:T(128)}, /*index=5*/f32[4]{0:T(128)}, f32[4]{0:T(...) fusion(f32[4,1024,1024]{2,1,0:T(8,128)} %get-tuple-element.285,, ...), kind=kLoop, calls=%fused_computation.311 | loop fusion | flops 150994912 | bytes 33554720 | tf_op jit(solution)/shard_map/while/body/eval_jaxpr/reduce_sum | solution.py:66
  2415.5 186.3 %multiply_reduce_fusion.18 = (f32[4]{0:T(128)}, f32[4]{0:T(128)}, f32[4]{0:T(128)}, f32[4]{0:T(128)}, f32[4]{0:T(128)}, /*index=5*/f32[4]{0:T(128)}, f32[4]{0:T(...) fusion(f32[4,1024,1024]{2,1,0:T(8,128)} %get-tuple-element.285,, ...), kind=kLoop, calls=%fused_computation.293 | loop fusion | flops 150994912 | bytes 33554720 | tf_op jit(solution)/shard_map/while/body/eval_jaxpr/reduce_sum | solution.py:66
  2604.4 174.2 %multiply_reduce_fusion = (f32[4]{0:T(128)}, f32[4]{0:T(128)}, f32[4]{0:T(128)}, f32[4]{0:T(128)}, f32[4]{0:T(128)}, /*index=5*/f32[4]{0:T(128)}, f32[4]{0:T(128...) fusion(f32[4,1024,1024]{2,1,0:T(8,128)} %get-tuple-element.285,, ...), kind=kLoop, calls=%fused_computation.275 | loop fusion | flops 150994912 | bytes 33554720 | tf_op jit(solution)/shard_map/while/body/eval_jaxpr/reduce_sum | solution.py:66
  2825.1 154.8 %fusion.174 = f32[2,2,2,1]{2,1,3,0:T(2,128)} fusion(f32[2,2,1024,1024]{2,1,3,0:T(2,128)} %copy.125, f32[2,2,1024,1024]{2,1,3,0:T(2,128)} %copy.126), kind=kOutput, calls=%fused_computation.495 | convolution fusion | flops 100663296 | bytes 33554464 | tf_op jit(solution)/shard_map/while/body/eval_jaxpr/grqk,gsqk->grs/dot_general | solution.py:91
  2992.5 38.2 %all-reduce.2 = (f32[384]{0:T(512)}, f32[4,6,11]{2,1,0:T(8,128)}, f32[4,2]{0,1:T(2,128)}, f32[384]{0:T(512)}, f32[384]{0:T(512)}) all-reduce(f32[384]{0:T(512)} %get-tuple-element.181, f32[4,6,11]{2,1,0:T(8,128)S(1)} %reduce_sum.848, f32[4,2]{0,1:T(2,128)} %copy.136, f32[384]{0:T(512)} %reshape.232, ...), channel_id=1, replica_groups=mesh['dp'=8,'tensor'=4] {'dp'}, use_global_device_ids=true, to_apply=%region_15.16 | all-reduce | flops 1424 | bytes 11392 | tf_op jit(solution)/shard_map/psum | solution.py:279
  3041.4 8.0 copy.129
  3049.4 12.6 copy.131
  (258 shorter events, 247.6 us)
Async XLA Ops:
  7.2 36.3 %copy-start = (bf16[3,1536,384]{2,1,0:T(8,128)(2,1)S(1)}, bf16[3,1536,384]{2,1,0:T(8,128)(2,1)}, u32[]{:S(2)}) copy-start(bf16[3,1536,384]{2,1,0:T(8,128)(2,1)} %param.15) | copy-start | bytes 10616836
  7.2 33.6 %all-gather.5.cloned.1.call-start = ((), (), s32[]{:S(2)}) async-start(), calls=%async_computation.2 | async-start | bytes 3932160 | tf_op jit(solution)/shard_map/all_gather | solution.py:165
  7.9 965.7 %all-reduce.8.cloned.1.call-start = ((), (), s32[]{:S(2)}) async-start(), calls=%async_computation.3 | async-start | bytes 12582912 | tf_op jit(solution)/shard_map/psum | solution.py:192
  11.0 39.6 %copy-start.35 = (f32[2,2,2]{1,0,2:T(2,128)}, f32[2,2,2]{1,0,2:T(2,128)S(1)}, u32[]{:S(2)}) copy-start(f32[2,2,2]{1,0,2:T(2,128)S(1)} %reshape.226) | copy-start | bytes 100
  43.5 15.8 copy-start.31
  836.8 11.3 copy-start.33
  836.9 12.4 copy-start.18
  853.9 150.0 %all-gather.7.cloned.1.call-start = ((), (), s32[]{:S(2)}) async-start(), calls=%async_computation.4 | async-start | bytes 3932160 | tf_op jit(solution)/shard_map/all_gather | solution.py:209
  854.6 293.0 %all-reduce.10.cloned.1.call-start = ((), (), s32[]{:S(2)}) async-start(), calls=%async_computation.5 | async-start | bytes 12582912 | tf_op jit(solution)/shard_map/psum | solution.py:221
  1027.9 1954.7 %reduce-scatter.7.cloned.1.call-start = ((), (), s32[]{:S(2)}) async-start(), calls=%async_computation.6 | async-start | bytes 3932160
  1035.9 111.7 %copy-start.27 = (f32[1536]{0:T(1024)S(1)}, f32[1536]{0:T(1024)}, u32[]{:S(2)}) copy-start(f32[1536]{0:T(1024)} %reshape.239) | copy-start | bytes 18436
  1035.9 111.7 %copy-start.30 = (f32[1024]{0:T(1024)S(1)}, f32[1024]{0:T(1024)}, u32[]{:S(2)}) copy-start(f32[1024]{0:T(1024)} %copy-done.29) | copy-start | bytes 12292
  1048.2 1939.4 %reduce-scatter.9.cloned.1.call-start = ((), (), s32[]{:S(2)}) async-start(), calls=%async_computation.7 | async-start | bytes 3932160
  1147.6 12.3 copy-start.19
  1166.3 11.2 copy-start.2
  1166.3 11.2 copy-start.28
  1166.3 11.2 copy-start.40
  1199.0 101.0 %copy-start.38 = (f32[4]{0:T(128)S(1)}, f32[4]{0:T(128)}, u32[]{:S(2)}) copy-start(f32[4]{0:T(128)} %get-tuple-element.204) | copy-start | bytes 52
  2115.0 926.4 %all-reduce.12.cloned.1.call-start = ((), (), s32[]{:S(2)}) async-start(), calls=%async_computation.8 | async-start | bytes 56623104 | tf_op jit(solution)/shard_map/psum | solution.py:279
  2115.1 23.1 slice-start
  2124.2 14.0 slice-start.1
  2124.2 14.0 copy-start.17
  2124.2 16.8 copy-start.9
  2124.2 16.8 copy-start.20
  2124.2 16.8 copy-start.21
  2124.2 16.8 copy-start.22
  2124.2 16.8 copy-start.32
  2124.2 16.8 copy-start.37
  2174.2 25.6 copy-start.36
  2174.2 26.2 copy-start.48
  2174.2 26.3 copy-start.47
  2174.2 26.4 copy-start.46
  (28 other events, 162.0 us)
Sparse Core Ops, SparseCore 0:
  9.6 31.1 all-gather.4
  854.0 119.5 all-reduce.7
  975.2 28.6 all-gather.6
  1028.0 119.5 all-reduce.9
  1150.0 38.1 reduce-scatter.6
  2115.1 37.7 reduce-scatter.8
  2159.0 836.7 all-reduce.11
where the time goes:
time: 3090 us; the launch traced here: 3080 us
  other arithmetic  2250 us (73%)
  matrix products  276 us (9%)
  local copies, waits for them, and re-layouts  249 us (8%)
  waiting for transfers between devices  232 us (8%)
  blocking collectives  55.1 us (2%)
    convert_element_type x1, other arithmetic, attend_backward(): (jnp.where(valid, grad_masked, 0.0) * scale).astype(jnp.bfloat16)  771 us
    reduce_max x1, other arithmetic, attend_forward(): peak = jnp.max(logits, axis=-1, keepdims=True)  755 us
    reduce_sum x3, other arithmetic, conv_back(): kernel_terms.append(jnp.sum(grad_logits * window_in, axis=(1, 2)))  541 us
    dot_general x1, matrix products, mix_back(): grad_mix = jnp.einsum('grqk,gsqk->grs', paired_grad, paired, precision=HIGH)  155 us
    psum x1, waiting for transfers between devices, on_device(): attn = lax.psum(attn_part, 'tensor')  111 us
    sub x1, other arithmetic, attend_backward(): grad_probs - jnp.sum(grad_probs * probs, axis=-1, keepdims=True)  101 us
    psum x1, waiting for transfers between devices, on_device(): grad_two = lax.psum(grad_two_part, 'tensor')  99.3 us
    another operation x67, local copies, waits for them, and re-layouts, conv_back(): jnp.stack(kernel_terms, axis=1).reshape(heads_here, query_taps, key_taps)  82.4 us
  transfers between devices with their start and end apart: 7, of which 4 were waited for; matrix products, arithmetic and copies ran while one was open for 62% of the time, Pallas kernels for 0%

commit v1 on v0

--- a/solution.py
+++ b/solution.py
@@ -218,7 +218,7 @@
     grad_two_part = jnp.einsum(
         "ctf,cdf->td", grad_pair, w_gate_up, preferred_element_type=jnp.float32
     )
-    grad_two = lax.psum(grad_two_part, "tensor")
+    grad_two = lax.all_gather(grad_two_part, axis_name="tensor").sum(axis=0)
     grad_gain_two = lax.dynamic_slice_in_dim(
         jnp.sum(grad_two * unit_two, axis=0), start, local_width, 0
     )

time: 3090 us -> 3180 us (1.029)
  other arithmetic: 2250 us -> 2310 us
  waiting for transfers between devices: 232 us -> 265 us
    all_gather x0 -> x1, waiting for transfers between devices: none -> 132 us  [on_device(): grad_two = lax.all_gather(grad_two_part, axis_name='tensor').sum(axis=0)]
    psum x1 -> x0, waiting for transfers between devices: 99.3 us -> none  [on_device(): grad_two = lax.psum(grad_two_part, 'tensor')]
    convert_element_type x1, other arithmetic: 771 us -> 804 us  [attend_backward(): (jnp.where(valid, grad_masked, 0.0) * scale).astype(jnp.bfloat16)]
  transfers between devices with their start and end apart: 7 -> 7, of which waited for: 4 -> 4; matrix products, arithmetic and copies ran while one was open for 62% -> 61% of each run, Pallas kernels for 0% -> 0%
where the time goes in v1:
time: 3180 us; the launch traced here: 3170 us
  other arithmetic  2310 us (73%)
  matrix products  278 us (9%)
  waiting for transfers between devices  265 us (8%)
  local copies, waits for them, and re-layouts  250 us (8%)
  blocking collectives  55.5 us (2%)
    convert_element_type x1, other arithmetic, attend_backward(): (jnp.where(valid, grad_masked, 0.0) * scale).astype(jnp.bfloat16)  804 us
    reduce_max x1, other arithmetic, attend_forward(): peak = jnp.max(logits, axis=-1, keepdims=True)  778 us
    reduce_sum x3, other arithmetic, conv_back(): kernel_terms.append(jnp.sum(grad_logits * window_in, axis=(1, 2)))  533 us
    dot_general x1, matrix products, mix_back(): grad_mix = jnp.einsum('grqk,gsqk->grs', paired_grad, paired, precision=HIGH)  155 us
    all_gather x1, waiting for transfers between devices, on_device(): grad_two = lax.all_gather(grad_two_part, axis_name='tensor').sum(axis=0)  132 us
    psum x1, waiting for transfers between devices, on_device(): attn = lax.psum(attn_part, 'tensor')  111 us
    sub x1, other arithmetic, attend_backward(): grad_probs - jnp.sum(grad_probs * probs, axis=-1, keepdims=True)  99.6 us
    another operation x67, local copies, waits for them, and re-layouts, conv_back(): jnp.stack(kernel_terms, axis=1).reshape(heads_here, query_taps, key_taps)  82.8 us
  transfers between devices with their start and end apart: 7, of which 4 were waited for; matrix products, arithmetic and copies ran while one was open for 61% of the time, Pallas kernels for 0%

profile of v1, /device:TPU:0, one launch (start us, length us, event | category | flops | bytes accessed | tf_op | source)
XLA Modules:
  0.0 3173.7 jit_solution(16991417739232420487)
XLA Ops:
  29.6 11.2 all-gather.7.cloned.1.call-done
  50.7 8.7 multiply_select_fusion
  59.4 777.6 %fusion.168 = (f32[4,1024]{1,0:T(4,128)S(1)}, f32[4,1024,1024]{2,1,0:T(8,128)}) fusion(f32[4]{0:T(128)} %get-tuple-element.249, f32[4]{0:T(128)} %get-tuple-element.250, f32[4]{0:T(128)} %get-tuple-element.186, f32[4]{0:T(128)} %get-tuple-element.187, f32[4]{0:T(128)} %get-tuple-element.188, f32[4]{0:T(128)} %get-tuple-element.189, ...), kind=kLoop, calls=%fused_computation.489 | loop fusion | flops 557838336 | bytes 34620448 | tf_op jit(solution)/shard_map/while/body/eval_jaxpr/reduce_max | solution.py:106
  837.0 7.8 fusion.140
  852.4 7.6 slice_bitcast_fusion.5
  860.0 7.4 fusion.138
  885.6 111.2 %all-reduce.7.cloned.1.call-done = f32[1024,1536]{1,0:T(8,128)} async-done(((f32[1024,1536]{1,0:T(8,128)}), f32[1024,1536]{1,0:T(8,128)}) %all-reduce.7.cloned.1.call-update) | async-done | bytes 6291472 | tf_op jit(solution)/shard_map/psum | solution.py:192
  996.8 7.6 multiply_reduce_fusion.68
  1007.3 11.3 convolution_bitcast_fusion.3
  1018.7 8.4 all-gather.9.cloned.1.call-done
  1027.1 11.5 fusion.147
  1040.6 10.5 convolution_bitcast_fusion.2
  1059.1 9.4 convolution_convert_fusion
  1073.8 132.4 %all-gather.11.cloned.1.call-done = f32[4096,1536]{1,0:T(8,128)} async-done(((f32[1024,1536]{1,0:T(8,128)}), f32[4096,1536]{1,0:T(8,128)}) %all-gather.11.cloned.1.call-update) | async-done | bytes 25165840 | tf_op jit(solution)/shard_map/all_gather | solution.py:221
  1206.1 13.9 reduce_sum.786
  1237.8 7.2 slice_bitcast_fusion.3
  1248.7 21.5 fusion.134
  1270.1 99.6 %multiply_reduce_fusion.54 = (f32[4]{0:T(128)}, f32[4]{0:T(128)}, f32[4]{0:T(128)}, f32[4]{0:T(128)}, f32[4]{0:T(128)}, /*index=5*/f32[4]{0:T(128)}, f32[4]{0:T(...) fusion(f32[4,1024,1024]{2,1,0:T(8,128)} %multiply_select_fusion, ...), kind=kOutput, calls=%fused_computation.329 | output fusion | flops 121639920 | bytes 83886304 | tf_op jit(solution)/shard_map/while/body/eval_jaxpr/sub | solution.py:123
  1369.8 804.2 %multiply_convert_fusion = bf16[4,1024,1024]{2,1,0:T(8,128)(2,1)} fusion(f32[4,1024,1024]{2,1,0:T(8,128)} %get-tuple-element.285, f32[4]{0:T(128)} %get-tuple-element.249, f32[4]{0:T(128)} %get-tuple-element.250, f32[4]{0:T(128)} %get-tuple-element.186, f32[4]{0:T(128)} %get-tuple-element.187, f32[4]{0:T(128)} %get-tuple-element.188, ...), kind=kLoop, calls=%fused_computation.341 | loop fusion | flops 562036736 | bytes 26215456 | tf_op jit(solution)/shard_map/while/body/eval_jaxpr/convert_element_type | solution.py:125
  2174.0 7.2 convolution_convert_fusion.3
  2206.0 7.3 bitcast_convert_fusion
  2218.1 9.0 fusion.175
  2227.1 14.1 convolution_bitcast_fusion
  2256.6 25.5 copy.125
  2282.2 25.5 copy.126
  2321.1 178.4 %multiply_reduce_fusion.36 = (f32[4]{0:T(128)}, f32[4]{0:T(128)}, f32[4]{0:T(128)}, f32[4]{0:T(128)}, f32[4]{0:T(128)}, /*index=5*/f32[4]{0:T(128)}, f32[4]{0:T(...) fusion(f32[4,1024,1024]{2,1,0:T(8,128)} %get-tuple-element.285,, ...), kind=kLoop, calls=%fused_computation.311 | loop fusion | flops 150994912 | bytes 33554720 | tf_op jit(solution)/shard_map/while/body/eval_jaxpr/reduce_sum | solution.py:66
  2522.9 183.7 %multiply_reduce_fusion.18 = (f32[4]{0:T(128)}, f32[4]{0:T(128)}, f32[4]{0:T(128)}, f32[4]{0:T(128)}, f32[4]{0:T(128)}, /*index=5*/f32[4]{0:T(128)}, f32[4]{0:T(...) fusion(f32[4,1024,1024]{2,1,0:T(8,128)} %get-tuple-element.285,, ...), kind=kLoop, calls=%fused_computation.293 | loop fusion | flops 150994912 | bytes 33554720 | tf_op jit(solution)/shard_map/while/body/eval_jaxpr/reduce_sum | solution.py:66
  2709.1 171.1 %multiply_reduce_fusion = (f32[4]{0:T(128)}, f32[4]{0:T(128)}, f32[4]{0:T(128)}, f32[4]{0:T(128)}, f32[4]{0:T(128)}, /*index=5*/f32[4]{0:T(128)}, f32[4]{0:T(128...) fusion(f32[4,1024,1024]{2,1,0:T(8,128)} %get-tuple-element.285,, ...), kind=kLoop, calls=%fused_computation.275 | loop fusion | flops 150994912 | bytes 33554720 | tf_op jit(solution)/shard_map/while/body/eval_jaxpr/reduce_sum | solution.py:66
  2926.5 154.8 %fusion.174 = f32[2,2,2,1]{2,1,3,0:T(2,128)} fusion(f32[2,2,1024,1024]{2,1,3,0:T(2,128)} %copy.125, f32[2,2,1024,1024]{2,1,3,0:T(2,128)} %copy.126), kind=kOutput, calls=%fused_computation.495 | convolution fusion | flops 100663296 | bytes 33554464 | tf_op jit(solution)/shard_map/while/body/eval_jaxpr/grqk,gsqk->grs/dot_general | solution.py:91
  3087.6 38.5 %all-reduce.2 = (f32[384]{0:T(512)}, f32[4,6,11]{2,1,0:T(8,128)}, f32[4,2]{0,1:T(2,128)}, f32[384]{0:T(512)}, f32[384]{0:T(512)}) all-reduce(f32[384]{0:T(512)} %get-tuple-element.181, f32[4,6,11]{2,1,0:T(8,128)S(1)} %reduce_sum.858, f32[4,2]{0,1:T(2,128)} %copy.136, f32[384]{0:T(512)} %reshape.232, ...), channel_id=1, replica_groups=mesh['dp'=8,'tensor'=4] {'dp'}, use_global_device_ids=true, to_apply=%region_15.16 | all-reduce | flops 1424 | bytes 11392 | tf_op jit(solution)/shard_map/psum | solution.py:279
  3136.9 8.0 copy.129
  3144.9 12.6 copy.131
  (259 shorter events, 254.0 us)
Async XLA Ops:
  7.2 36.3 %copy-start = (bf16[3,1536,384]{2,1,0:T(8,128)(2,1)S(1)}, bf16[3,1536,384]{2,1,0:T(8,128)(2,1)}, u32[]{:S(2)}) copy-start(bf16[3,1536,384]{2,1,0:T(8,128)(2,1)} %param.15) | copy-start | bytes 10616836
  7.2 33.6 %all-gather.7.cloned.1.call-start = ((), (), s32[]{:S(2)}) async-start(), calls=%async_computation.2 | async-start | bytes 3932160 | tf_op jit(solution)/shard_map/all_gather | solution.py:165
  7.9 988.9 %all-reduce.7.cloned.1.call-start = ((), (), s32[]{:S(2)}) async-start(), calls=%async_computation.3 | async-start | bytes 12582912 | tf_op jit(solution)/shard_map/psum | solution.py:192
  11.0 39.6 %copy-start.35 = (f32[2,2,2]{1,0,2:T(2,128)}, f32[2,2,2]{1,0,2:T(2,128)S(1)}, u32[]{:S(2)}) copy-start(f32[2,2,2]{1,0,2:T(2,128)S(1)} %reshape.226) | copy-start | bytes 100
  43.5 15.9 copy-start.31
  860.0 11.3 copy-start.33
  860.0 12.4 copy-start.18
  877.1 150.0 %all-gather.9.cloned.1.call-start = ((), (), s32[]{:S(2)}) async-start(), calls=%async_computation.4 | async-start | bytes 3932160 | tf_op jit(solution)/shard_map/all_gather | solution.py:209
  877.8 328.3 %all-gather.11.cloned.1.call-start = ((), (), s32[]{:S(2)}) async-start(), calls=%async_computation.5 | async-start | bytes 31457280 | tf_op jit(solution)/shard_map/all_gather | solution.py:221
  1051.1 1200.5 %reduce-scatter.7.cloned.1.call-start = ((), (), s32[]{:S(2)}) async-start(), calls=%async_computation.6 | async-start | bytes 3932160
  1073.7 146.3 %copy-start.27 = (f32[1536]{0:T(1024)S(1)}, f32[1536]{0:T(1024)}, u32[]{:S(2)}) copy-start(f32[1536]{0:T(1024)} %reshape.240) | copy-start | bytes 18436
  1073.7 146.3 %copy-start.30 = (f32[1024]{0:T(1024)S(1)}, f32[1024]{0:T(1024)}, u32[]{:S(2)}) copy-start(f32[1024]{0:T(1024)} %copy-done.29) | copy-start | bytes 12292
  1073.7 2009.0 %reduce-scatter.9.cloned.1.call-start = ((), (), s32[]{:S(2)}) async-start(), calls=%async_computation.7 | async-start | bytes 3932160
  1220.0 11.4 copy-start.19
  1237.8 10.9 copy-start.2
  1237.8 10.9 copy-start.28
  1237.8 10.9 copy-start.40
  1270.1 99.6 %copy-start.38 = (f32[4]{0:T(128)S(1)}, f32[4]{0:T(128)}, u32[]{:S(2)}) copy-start(f32[4]{0:T(128)} %get-tuple-element.204) | copy-start | bytes 52
  2218.0 918.8 %all-reduce.9.cloned.1.call-start = ((), (), s32[]{:S(2)}) async-start(), calls=%async_computation.8 | async-start | bytes 56623104 | tf_op jit(solution)/shard_map/psum | solution.py:279
  2218.1 23.1 slice-start
  2227.1 14.1 slice-start.1
  2227.1 14.1 copy-start.17
  2227.1 16.9 copy-start.9
  2227.1 16.9 copy-start.20
  2227.1 16.9 copy-start.21
  2227.1 16.9 copy-start.22
  2227.1 16.9 copy-start.32
  2227.1 16.9 copy-start.37
  2282.2 26.8 copy-start.36
  2282.2 27.5 copy-start.48
  2282.2 27.6 copy-start.47
  2282.2 27.7 copy-start.46
  (28 other events, 158.1 us)
Sparse Core Ops, SparseCore 0:
  9.6 31.1 all-gather.6
  877.2 119.5 all-reduce.6
  998.4 28.6 all-gather.8
  1051.2 154.8 all-gather.10
  1208.5 37.9 reduce-scatter.6
  2218.1 38.4 reduce-scatter.8
  2262.6 836.8 all-reduce.8
